TPU v7x, 32 devices: a whole 2x2x4 slice. The times are simulated.
32 devices in a mesh: row: 16 (over z, y, core), col: 2 (over x).
Axes of the slice: x: 2, y: 2, z: 4, core: 2. Of those that a mesh axis runs over, the one named last changes fastest.
Arguments:
- samples: float32 [256, 16384], P(None, 'col'), may hold values from -0.8 to 0.8
- values: float32 [16384, 16384], P('row', 'col'), may hold values from -6 to 6
- diag_entries: float32 [16384], P('row'), may hold values from 16 to 32
- block_mask: int32 [64, 64], replicated, may hold values 0 or 1
Outputs:
- updated: float32 [16384, 16384], P('row', 'col')
All inputs are finite; a program needn't handle non-finite values.
Results may differ from a plain program's by a relative error of at most 0.0003.
Values sent between devices are 32-bit elements; how exact they have to be, the bound alone decides.
A program may use at most 192 MiB of HBM per device.

v0:
```python
import jax
import jax.numpy as jnp
from jax import lax
from jax.sharding import PartitionSpec as P

step_size = 8.0
penalty = 0.05


def per_device(samples, values, diag_entries, block_mask):
    tile_rows = values.shape[0]
    tile_cols = values.shape[1]
    sample_count = samples.shape[0]
    order_total = lax.axis_size("col") * tile_cols
    per_group = tile_cols // tile_rows
    row_index = lax.axis_index("row")
    owner_col = row_index // per_group
    is_owner = lax.axis_index("col") == owner_col
    slice_at = row_index % per_group * tile_rows
    mask_block = order_total // block_mask.shape[0]
    row_at = row_index * tile_rows
    col_at = lax.axis_index("col") * tile_cols
    mask_rows = tile_rows // mask_block
    mask_cols = tile_cols // mask_block
    tile_mask = lax.dynamic_slice(
        block_mask, (row_at // mask_block, col_at // mask_block), (mask_rows, mask_cols)
    )
    mask_grid = tile_mask.astype(jnp.float32)[:, None, :, None]
    expanded = jnp.broadcast_to(mask_grid, (mask_rows, mask_block, mask_cols, mask_block)).reshape(
        tile_rows, tile_cols
    )
    row_ids = row_at + jnp.arange(tile_rows, dtype=jnp.int32)
    col_ids = col_at + jnp.arange(tile_cols, dtype=jnp.int32)
    on_diag = row_ids[:, None] == col_ids[None, :]
    omega_tile = jnp.where(on_diag, diag_entries[:, None], expanded * values)
    local_cols = lax.dynamic_slice_in_dim(samples, slice_at, tile_rows, 1)
    owned_cols = jnp.where(is_owner, local_cols, jnp.float32(0.0))
    row_samples = lax.psum(owned_cols, "col")
    partial_value = jnp.dot(
        row_samples, omega_tile, precision=lax.Precision.HIGHEST, preferred_element_type=jnp.float32
    )
    summed = lax.psum(partial_value, "row")
    product = lax.dot_general(
        row_samples,
        summed,
        (((0,), (0,)), ((), ())),
        precision=lax.Precision.HIGHEST,
        preferred_element_type=jnp.float32,
    )
    product = product / sample_count
    local_proj = lax.dynamic_slice_in_dim(summed, slice_at, tile_rows, 1)
    owned_proj = jnp.where(is_owner, local_proj, jnp.float32(0.0))
    row_proj = lax.psum(owned_proj, "col")
    mirrored = lax.dot_general(
        row_proj,
        samples,
        (((0,), (0,)), ((), ())),
        precision=lax.Precision.HIGHEST,
        preferred_element_type=jnp.float32,
    )
    mirrored = mirrored / sample_count
    gradient = 0.5 * (product + mirrored) - jnp.where(
        on_diag, 1.0 / diag_entries[:, None], jnp.float32(0.0)
    )
    stepped = omega_tile - step_size * gradient
    shrunk = jnp.sign(stepped) * jnp.maximum(
        jnp.abs(stepped) - step_size * penalty, jnp.float32(0.0)
    )
    return jnp.where(on_diag, stepped, shrunk)


def solution(mesh):
    in_specs = (P(None, "col"), P("row", "col"), P("row"), P())
    out_specs = P("row", "col")
    return jax.shard_map(
        per_device, mesh=mesh, in_specs=in_specs, out_specs=out_specs, check_vma=False
    )
```

profile of v0, /device:TPU:30, one launch (start us, length us, event | category | flops | bytes accessed | tf_op | source)
XLA Modules:
  0.0 369.4 jit_solution(9567092727064059548)
XLA Ops:
  6.5 0.0 all-reduce.4.cloned.1.call-start
  6.5 2.3 dynamic-slice_select_fusion.1
  8.8 0.0 all-reduce.4.cloned.1.call-update
  8.9 0.0 all-reduce.6.cloned.1.call-start
  9.0 0.8 dynamic-slice_convert_fusion
  9.7 4.8 %broadcast_in_dim.36 = f32[4,256,32,256]{3,2,1,0:T(8,128)S(1)} broadcast(f32[4,32]{1,0:T(4,128)S(1)} %dynamic-slice_convert_fusion), dimensions={0,2} | broadcast | bytes 33554944 | tf_op jit(solution)/shard_map/broadcast_in_dim | solution.py:29
  14.6 0.0 copy-start.1
  14.6 34.1 %copy.5 = f32[128,8,32,256]{3,1,2,0:T(8,128)} copy(f32[128,8,32,256]{3,2,1,0:T(8,128)S(1)} %bitcast.10) | data formatting | bytes 67108864
  48.7 1.1 all-reduce.4.cloned.1.call-done
  49.8 0.0 copy-done.1
  49.8 0.0 copy-start
  49.8 38.5 %fusion.3 = f32[256,8192]{1,0:T(8,128)} fusion(f32[256,1024]{1,0:T(8,128)} %all-reduce.4.cloned.1.call-done, f32[1024,8192]{1,0:T(8,128)} %bitcast.8, f32[1024,8192]{1,0:T(8,128)} %param.5, f32[1024]{0:T(1024)S(1)} %copy-done.1, s32[8192]{0:T(1024)S(1)} %iota_add_fusion, s32[1024]{0:T(1024)S(1)} %iota_add_fusion.1), kind=kOutput, calls=%fused_computation.12 | convolution fusion | flops 25794969600 | bytes 76587008 | tf_op jit(solution)/shard_map/dot_general | solution.py:39
  88.3 0.0 all-reduce.6.cloned.1.call-update
  88.4 0.2 all-reduce.8.cloned.1.call-start
  88.6 169.9 %all-reduce.6.cloned.1.call-done = f32[256,8192]{1,0:T(8,128)} async-done(((f32[256,8192]{1,0:T(8,128)}), f32[256,8192]{1,0:T(8,128)}) %all-reduce.6.cloned.1.call-update) | async-done | bytes 8388624 | tf_op jit(solution)/shard_map/psum | solution.py:42
  258.5 2.4 dynamic-slice_select_fusion
  260.8 0.0 all-reduce.8.cloned.1.call-update
  260.8 0.0 copy-done
  260.8 31.9 %fusion.4 = f32[1024,8192]{1,0:T(8,128)} fusion(f32[256,1024]{1,0:T(8,128)S(1)} %copy-done, f32[256,8192]{1,0:T(8,128)} %all-reduce.6.cloned.1.call-done), kind=kOutput, calls=%fused_computation.13 | convolution fusion | flops 25769803776 | bytes 42991616 | tf_op jit(solution)/shard_map/dot_general | solution.py:43
  292.8 8.3 %all-reduce.8.cloned.1.call-done = f32[256,1024]{1,0:T(8,128)} async-done(((f32[256,1024]{1,0:T(8,128)}), f32[256,1024]{1,0:T(8,128)}) %all-reduce.8.cloned.1.call-update) | async-done | bytes 1048592 | tf_op jit(solution)/shard_map/psum | solution.py:53
  301.1 61.8 %compare_select_fusion = f32[1024,8192]{1,0:T(8,128)} fusion(f32[1024,8192]{1,0:T(8,128)} %fusion.4, f32[256,1024]{1,0:T(8,128)} %all-reduce.8.cloned.1.call-done, f32[256,8192]{1,0:T(8,128)} %param.4, f32[1024]{0:T(1024)S(1)} %broadcast_divide_fusion, s32[8192]{0:T(1024)S(1)} %iota_add_fusion, s32[1024]{0:T(1024)S(1)} %iota_add_fusion.1, ...), kind=kOutput, calls=%fused_computation | convolution fusion | flops 25895632896 | bytes 143699968 | tf_op jit(solution)/shard_map/dot_general | solution.py:54
  (3 shorter events, 0.0 us)
Async XLA Ops:
  6.5 43.3 %all-reduce.4.cloned.1.call-start = ((), (), s32[]{:S(2)}) async-start(), calls=%async_computation | async-start | bytes 2097152 | tf_op jit(solution)/shard_map/psum | solution.py:38
  8.9 249.6 %all-reduce.6.cloned.1.call-start = ((), (), s32[]{:S(2)}) async-start(), calls=%async_computation.1 | async-start | bytes 16777216 | tf_op jit(solution)/shard_map/psum | solution.py:42
  14.6 35.2 %copy-start.1 = (f32[1024]{0:T(1024)S(1)}, f32[1024]{0:T(1024)}, u32[]{:S(2)}) copy-start(f32[1024]{0:T(1024)} %param.6) | copy-start | bytes 12292
  49.8 211.0 %copy-start = (f32[256,1024]{1,0:T(8,128)S(1)}, f32[256,1024]{1,0:T(8,128)}, u32[]{:S(2)}) copy-start(f32[256,1024]{1,0:T(8,128)} %all-reduce.4.cloned.1.call-done) | copy-start | bytes 3145732
  88.4 212.7 %all-reduce.8.cloned.1.call-start = ((), (), s32[]{:S(2)}) async-start(), calls=%async_computation.2 | async-start | bytes 2097152 | tf_op jit(solution)/shard_map/psum | solution.py:53
Sparse Core Ops, SparseCore 0:
  9.6 40.1 all-reduce.3
  88.5 169.9 all-reduce.5
  260.9 40.0 all-reduce.7
where the time goes:
time: 372 us; the launch traced here: 369 us
  waiting for transfers between devices  179 us (48%)
  matrix products  132 us (35%)
  local copies, waits for them, and re-layouts  38.9 us (10%)
  between operations  13.2 us (4%)
  other arithmetic  5.44 us (1%)
    psum x1, waiting for transfers between devices, per_device(): summed = lax.psum(partial_value, 'row')  170 us
    dot_general x1, matrix products, per_device(): lax.dot_general(row_proj, samples, (((0,), (0,)), ((), ())), precision=la...  61.8 us
    dot_general x1, matrix products, per_device(): jnp.dot(row_samples, omega_tile, precision=lax.Precision.HIGHEST, preferr...  38.5 us
    unnamed x5, local copies, waits for them, and re-layouts  34.1 us
    dot_general x1, matrix products, per_device(): lax.dot_general(row_samples, summed, (((0,), (0,)), ((), ())), precision=...  31.9 us
    psum x1, waiting for transfers between devices, per_device(): row_proj = lax.psum(owned_proj, 'col')  8.34 us
  transfers between devices with their start and end apart: 3, of which 3 were waited for; matrix products, arithmetic and copies ran while one was open for 19% of the time, Pallas kernels for 0%

commit v1 on v0

v1 whole, which is shorter than its diff:
```python
import functools

import jax
import jax.numpy as jnp
from jax import lax
from jax.experimental import pallas as pl
from jax.experimental.pallas import tpu as pltpu
from jax.sharding import PartitionSpec as P

step_size = 8.0
penalty = 0.05
MESH = pl.DeviceIdType.MESH
VM = pltpu.VMEM
LIMIT = 60 * 1024 * 1024


def split(x):
    high = x.astype(jnp.bfloat16)
    low = (x - high.astype(jnp.float32)).astype(jnp.bfloat16)
    return high, low


def dot(a, b):
    return jnp.dot(a, b, preferred_element_type=jnp.float32)


def fetch_kernel(groups, per_group, samples_ref, out_ref, local_sem, send_sem, recv_sem):
    row, col = lax.axis_index("row"), lax.axis_index("col")
    owner = row // per_group
    width = out_ref.shape[1]
    at = pl.multiple_of(row % per_group * width, width)
    source = samples_ref.at[:, pl.ds(at, width)]
    barrier = pltpu.get_barrier_semaphore()
    for shift in range(1, groups):
        pl.semaphore_signal(
            barrier, inc=1, device_id=(row, lax.rem(col + shift, groups)), device_id_type=MESH
        )
    pl.semaphore_wait(barrier, groups - 1)

    def remote(shift):
        return pltpu.make_async_remote_copy(
            src_ref=source,
            dst_ref=out_ref,
            send_sem=send_sem.at[shift],
            recv_sem=recv_sem,
            device_id=(row, lax.rem(col + shift, groups)),
            device_id_type=MESH,
        )

    @pl.when(col == owner)
    def _():
        for shift in range(1, groups):
            remote(shift).start()
        own = pltpu.make_async_copy(source, out_ref, local_sem)
        own.start()
        own.wait()
        for shift in range(1, groups):
            remote(shift).wait_send()

    @pl.when(col != owner)
    def _():
        remote(1).wait_recv()


def project_kernel(offset_ref, rows_ref, values_ref, diag_ref, mask_ref, out_ref, high_ref, low_ref):
    step = pl.program_id(0)
    tile = values_ref.shape[1]
    parts = mask_ref.shape[0]
    height = values_ref.shape[0] // parts

    @pl.when(step == 0)
    def _():
        high_ref[...], low_ref[...] = split(rows_ref[...])

    total = None
    for part in range(parts):
        begin = part * height
        rows = pl.ds(begin, height)
        omega = omega_tile(offset_ref, values_ref, diag_ref, mask_ref, step, part)
        high, low = split(omega)
        left = high_ref[:, rows]
        term = dot(left, high) + dot(low_ref[:, rows], high) + dot(left, low)
        total = term if total is None else total + term
    out_ref[...] = total


def on_diagonal(offset_ref, step, begin, shape):
    rows = lax.broadcasted_iota(jnp.int32, shape, 0) + (offset_ref[0] + begin)
    cols = lax.broadcasted_iota(jnp.int32, shape, 1) + (offset_ref[1] + step * shape[1])
    return rows == cols


def omega_tile(offset_ref, values_ref, diag_ref, mask_ref, step, part):
    height = values_ref.shape[0] // mask_ref.shape[0]
    rows = pl.ds(part * height, height)
    masked = values_ref[rows, :] * mask_ref[part : part + 1, :]
    diagonal = on_diagonal(offset_ref, step, part * height, masked.shape)
    return jnp.where(diagonal, diag_ref[rows, :], masked)


def update_kernel(
    offset_ref, left_ref, proj_ref, samples_ref, values_ref, diag_ref, mask_ref, out_ref, left_high, left_low, high_ref, low_ref
):
    step = pl.program_id(0)
    count = samples_ref.shape[0]
    parts = mask_ref.shape[0]
    height = values_ref.shape[0] // parts

    @pl.when(step == 0)
    def _():
        left_high[...], left_low[...] = split(left_ref[...])

    high_ref[:count, :], low_ref[:count, :] = split(proj_ref[...])
    high_ref[count:, :], low_ref[count:, :] = split(samples_ref[...])
    for part in range(parts):
        rows = pl.ds(part * height, height)
        cross = (
            dot(left_high[rows, :], high_ref[...])
            + dot(left_low[rows, :], high_ref[...])
            + dot(left_high[rows, :], low_ref[...])
        )
        diagonal = on_diagonal(offset_ref, step, part * height, cross.shape)
        diag = diag_ref[rows, :]
        omega = jnp.where(diagonal, diag, values_ref[rows, :] * mask_ref[part : part + 1, :])
        stepped = omega - cross * (0.5 * step_size / count)
        limit = step_size * penalty
        shrunk = stepped - jnp.clip(stepped, -limit, limit)
        out_ref[rows, :] = jnp.where(diagonal, stepped + step_size / diag, shrunk)


def reduce_kernel(lines, groups, per_group, chunks, part_ref, out_ref, proj_ref, *scratch):
    (core_in, y_in, a_right, a_left, b_right, b_left, y_right, y_left) = scratch[:8]
    send, recv = scratch[8], scratch[9]
    row, col = lax.axis_index("row"), lax.axis_index("col")
    core, side, line = row % 2, row // 2 % 2, row // 4
    last = lines - 1
    core_mate = row + 1 - 2 * core
    y_mate = row + 2 - 4 * side
    up, down = row + 4, row - 4
    samples, order = part_ref.shape
    deep = samples // chunks
    half, quarter, eighth, sixteenth = order // 2, order // 4, order // 8, order // 16
    has_up, has_down = line < last, line > 0
    owner = row // per_group
    width = proj_ref.shape[1]
    slice_at = pl.multiple_of(row % per_group * width, width)

    barrier = pltpu.get_barrier_semaphore()

    def greet(target):
        pl.semaphore_signal(barrier, inc=1, device_id=target, device_id_type=MESH)

    greet((core_mate, col))
    greet((y_mate, col))
    pl.when(has_up)(lambda: greet((up, col)))
    pl.when(has_down)(lambda: greet((down, col)))
    for shift in range(1, groups):
        greet((row, lax.rem(col + shift, groups)))
    ends = jnp.where(has_up, 1, 0) + jnp.where(has_down, 1, 0)
    pl.semaphore_wait(barrier, 2 + groups - 1 + ends)

    def span(at, size):
        return pl.ds(pl.multiple_of(at, sixteenth), size)

    def rows_of(q):
        return pl.ds(pl.multiple_of(q * deep, deep), deep)

    def a_at(k, v):
        return k * half + v * eighth

    def b_at(k):
        return k * half + quarter

    def copy(kind, q, source, target, device, landing=None):
        return pltpu.make_async_remote_copy(
            src_ref=source,
            dst_ref=target,
            send_sem=send.at[kind, q],
            recv_sem=recv.at[kind if landing is None else landing, q],
            device_id=device,
            device_id_type=MESH,
        )

    def whole(ref, q):
        return ref.at[rows_of(q), :]

    def out_at(q, at, size):
        return out_ref.at[rows_of(q), span(at, size)]

    def c_core(q):
        return copy(0, q, part_ref.at[rows_of(q), span((1 - core) * half, half)], whole(core_in, q), (core_mate, col))

    def c_y(q):
        return copy(1, q, core_in.at[rows_of(q), span((1 - side) * eighth, eighth)], whole(y_in, q), (y_mate, col))

    def c_b_right(q, first):
        source = core_in.at[rows_of(q), span(quarter, eighth)] if first else whole(b_right, q)
        return copy(2, q, source, whole(b_right, q), (up, col))

    def c_b_left(q, first):
        source = core_in.at[rows_of(q), span(quarter + eighth, eighth)] if first else whole(b_left, q)
        return copy(3, q, source, whole(b_left, q), (down, col))

    def c_a_right(q, first):
        source = y_in.at[rows_of(q), span(0, sixteenth)] if first else whole(a_right, q)
        return copy(4, q, source, whole(a_right, q), (up, col))

    def c_a_left(q, first):
        source = y_in.at[rows_of(q), span(sixteenth, sixteenth)] if first else whole(a_left, q)
        return copy(5, q, source, whole(a_left, q), (down, col))

    def c_y_right(q):
        return copy(6, q, whole(b_right, q), whole(y_right, q), (y_mate, col))

    def c_y_left(q):
        return copy(7, q, whole(b_left, q), whole(y_left, q), (y_mate, col))

    def spread(kind, q, at, size, target):
        return copy(kind, q, out_at(q, at, size), out_at(q, at, size), (target, col))

    def b_piece(flow):
        return b_at(core) + flow * eighth, eighth

    def a_piece(flow, v):
        return a_at(core, v) + flow * sixteenth, sixteenth

    def c_b_back(q, flow):
        return spread(8 + flow, q, *b_piece(flow), (down, up)[flow])

    def c_a_back(q, flow):
        return spread(10 + flow, q, *a_piece(flow, side), (down, up)[flow])

    def c_y_back(q, flow):
        return spread(12 + flow, q, *a_piece(flow, side), y_mate)

    def y_back_arrival(q, flow):
        return spread(12 + flow, q, *a_piece(flow, 1 - side), y_mate)

    def c_core_back(q, index, at, size):
        return copy(14 + index, q, out_at(q, at, size), out_at(q, at, size), (core_mate, col), 14 + index)

    def core_arrival(q, index, at, size):
        other = at - core * half + (1 - core) * half
        return c_core_back(q, index, other, size)

    pieces = []
    for flow in range(2):
        pieces += [(flow, *b_piece(flow)), (2 + flow, *a_piece(flow, side)), (4 + flow, *a_piece(flow, 1 - side))]

    def core_pieces_in(q):
        for flow in range(2):
            core_arrival(q, flow, *b_piece(flow)).wait_recv()
            for index, v in ((2, side), (4, 1 - side)):
                core_arrival(q, index + flow, *a_piece(flow, v)).wait_recv()

    def c_proj(q, shift):
        return copy(
            20 + shift,
            q,
            out_ref.at[rows_of(q), pl.ds(slice_at, width)],
            whole(proj_ref, q),
            (row, lax.rem(col + shift, groups)),
            21,
        )

    def at_stage(t, offset, condition, action):
        q = t - offset
        live = jnp.logical_and(q >= 0, q < chunks)
        if condition is not None:
            live = jnp.logical_and(live, condition)
        pl.when(live)(lambda: action(jnp.clip(q, 0, chunks - 1)))

    def begin(q):
        c_core(q).wait_recv()
        rows = rows_of(q)
        core_in[rows, :] = core_in[rows, :] + part_ref[rows, span(core * half, half)]
        c_y(q).start()
        pl.when(line == 0)(lambda: c_b_right(q, True).start())
        pl.when(line == last)(lambda: c_b_left(q, True).start())

    def after_y(q):
        c_y(q).wait_recv()
        rows = rows_of(q)
        y_in[rows, :] = y_in[rows, :] + core_in[rows, span(side * eighth, eighth)]
        pl.when(line == 0)(lambda: c_a_right(q, True).start())
        pl.when(line == last)(lambda: c_a_left(q, True).start())

    def b_hop(q, flow):
        ref, make = (b_right, c_b_right) if flow == 0 else (b_left, c_b_left)
        make(q, False).wait_recv()
        rows = rows_of(q)
        ref[rows, :] = ref[rows, :] + core_in[rows, span(quarter + flow * eighth, eighth)]
        going = has_up if flow == 0 else has_down
        pl.when(going)(lambda: make(q, False).start())
        pl.when(jnp.logical_not(going))(lambda: (c_y_right if flow == 0 else c_y_left)(q).start())

    def done_a(q, flow, forward):
        pl.when(forward)(lambda: c_a_back(q, flow).start())
        c_y_back(q, flow).start()
        c_core_back(q, 2 + flow, *a_piece(flow, side)).start()

    def done_b(q, flow, forward):
        pl.when(forward)(lambda: c_b_back(q, flow).start())
        c_core_back(q, flow, *b_piece(flow)).start()

    def a_hop(q, flow):
        ref, make = (a_right, c_a_right) if flow == 0 else (a_left, c_a_left)
        make(q, False).wait_recv()
        rows = rows_of(q)
        value = ref[rows, :] + y_in[rows, span(flow * sixteenth, sixteenth)]
        going = has_up if flow == 0 else has_down

        @pl.when(going)
        def _():
            ref[rows, :] = value
            make(q, False).start()

        @pl.when(jnp.logical_not(going))
        def _():
            out_ref[rows, span(*a_piece(flow, side))] = value
            done_a(q, flow, True)

    def b_end(q, flow):
        ref, other, make = (b_right, y_right, c_y_right) if flow == 0 else (b_left, y_left, c_y_left)
        make(q).wait_recv()
        rows = rows_of(q)
        out_ref[rows, span(*b_piece(flow))] = ref[rows, :] + other[rows, :]
        done_b(q, flow, True)

    def back(q, flow):
        forward = has_down if flow == 0 else has_up
        c_a_back(q, flow).wait_recv()
        done_a(q, flow, forward)
        c_b_back(q, flow).wait_recv()
        done_b(q, flow, forward)

    def y_gather(q, flow):
        y_back_arrival(q, flow).wait_recv()
        c_core_back(q, 4 + flow, *a_piece(flow, 1 - side)).start()

    def finish(q):
        core_pieces_in(q)
        rows = rows_of(q)

        @pl.when(col == owner)
        def _():
            for shift in range(1, groups):
                c_proj(q, shift).start()
            proj_ref[rows, :] = out_ref[rows, pl.ds(slice_at, width)]

    @pl.loop(0, chunks)
    def _(q):
        c_core(q).start()

    total = 2 * lines + 2

    @pl.loop(0, chunks + total)
    def _(t):
        at_stage(t, 0, None, begin)
        at_stage(t, 1, None, after_y)
        at_stage(t, line, has_down, lambda q: b_hop(q, 0))
        at_stage(t, last - line, has_up, lambda q: b_hop(q, 1))
        at_stage(t, 1 + line, has_down, lambda q: a_hop(q, 0))
        at_stage(t, lines - line, has_up, lambda q: a_hop(q, 1))
        at_stage(t, lines, line == last, lambda q: b_end(q, 0))
        at_stage(t, lines, line == 0, lambda q: b_end(q, 1))
        at_stage(t, lines + last - line, has_up, lambda q: back(q, 0))
        at_stage(t, lines + line, has_down, lambda q: back(q, 1))
        at_stage(t, lines + last - line + 1, None, lambda q: y_gather(q, 0))
        at_stage(t, lines + line + 1, None, lambda q: y_gather(q, 1))
        at_stage(t, 2 * lines + 1, None, finish)

    @pl.loop(0, chunks)
    def _(q):
        c_core(q).wait_send()
        c_y(q).wait_send()
        pl.when(has_up)(lambda: c_b_right(q, False).wait_send())
        pl.when(has_down)(lambda: c_b_left(q, False).wait_send())
        pl.when(has_up)(lambda: c_a_right(q, False).wait_send())
        pl.when(has_down)(lambda: c_a_left(q, False).wait_send())
        pl.when(line == last)(lambda: c_y_right(q).wait_send())
        pl.when(line == 0)(lambda: c_y_left(q).wait_send())
        for flow, forward in ((0, has_down), (1, has_up)):
            pl.when(forward)(lambda flow=flow: c_b_back(q, flow).wait_send())
            pl.when(forward)(lambda flow=flow: c_a_back(q, flow).wait_send())
            c_y_back(q, flow).wait_send()
        for index, at, size in pieces:
            c_core_back(q, index, at, size).wait_send()

        @pl.when(col == owner)
        def _():
            for shift in range(1, groups):
                c_proj(q, shift).wait_send()

        @pl.when(col != owner)
        def _():
            c_proj(q, 1).wait_recv()


def per_device(samples, values, diag_entries, block_mask):
    height, order = values.shape
    count = samples.shape[0]
    groups = lax.axis_size("col")
    lines = lax.axis_size("row") // 4
    per_group = order // height
    row_at = lax.axis_index("row") * height
    col_at = lax.axis_index("col") * order
    block = groups * order // block_mask.shape[0]
    tile_mask = lax.dynamic_slice(
        block_mask, (row_at // block, col_at // block), (height // block, order // block)
    )
    mask = jnp.repeat(tile_mask.astype(jnp.float32), block, axis=1)
    diag = diag_entries[:, None]
    offsets = jnp.stack([row_at, col_at]).astype(jnp.int32)
    anywhere = pl.BlockSpec(memory_space=pl.ANY)
    in_vmem = pl.BlockSpec(memory_space=VM)
    row_samples = pl.pallas_call(
        functools.partial(fetch_kernel, groups, per_group),
        out_shape=jax.ShapeDtypeStruct((count, height), jnp.float32),
        in_specs=[anywhere],
        out_specs=in_vmem,
        scratch_shapes=[
            pltpu.SemaphoreType.DMA,
            pltpu.SemaphoreType.DMA((groups,)),
            pltpu.SemaphoreType.DMA,
        ],
        compiler_params=pltpu.CompilerParams(collective_id=0, has_side_effects=True),
    )(samples)

    tile = 2 * block
    grid = order // tile
    fixed = lambda shape: pl.BlockSpec(shape, lambda i, s: (0, 0))
    moving = lambda rows: pl.BlockSpec((rows, tile), lambda i, s: (0, i))
    parts = mask.shape[0]
    partial_value = pl.pallas_call(
        project_kernel,
        out_shape=jax.ShapeDtypeStruct((count, order), jnp.float32),
        grid_spec=pltpu.PrefetchScalarGridSpec(
            num_scalar_prefetch=1,
            grid=(grid,),
            in_specs=[fixed((count, height)), moving(height), fixed((height, 1)), moving(parts)],
            out_specs=moving(count),
            scratch_shapes=[VM((count, height), jnp.bfloat16)] * 2,
        ),
        compiler_params=pltpu.CompilerParams(dimension_semantics=("arbitrary",), vmem_limit_bytes=LIMIT),
    )(offsets, row_samples, values, diag, mask)

    chunks = max(1, min(8, count // 8))
    eighth, sixteenth = order // 8, order // 16
    widths = [order // 2, eighth, sixteenth, sixteenth, eighth, eighth, eighth, eighth]
    kinds = 21 + groups
    projected, row_proj = pl.pallas_call(
        functools.partial(reduce_kernel, lines, groups, per_group, chunks),
        out_shape=(
            jax.ShapeDtypeStruct((count, order), jnp.float32),
            jax.ShapeDtypeStruct((count, height), jnp.float32),
        ),
        in_specs=[in_vmem],
        out_specs=(in_vmem, in_vmem),
        scratch_shapes=[VM((count, w), jnp.float32) for w in widths]
        + [pltpu.SemaphoreType.DMA((kinds, chunks)), pltpu.SemaphoreType.DMA((kinds, chunks))],
        compiler_params=pltpu.CompilerParams(
            collective_id=1, has_side_effects=True, vmem_limit_bytes=LIMIT
        ),
    )(partial_value)

    left = jnp.concatenate([row_samples, row_proj], axis=0).T
    return pl.pallas_call(
        update_kernel,
        out_shape=jax.ShapeDtypeStruct((height, order), jnp.float32),
        grid_spec=pltpu.PrefetchScalarGridSpec(
            num_scalar_prefetch=1,
            grid=(grid,),
            in_specs=[
                fixed((height, 2 * count)),
                moving(count),
                moving(count),
                moving(height),
                fixed((height, 1)),
                moving(parts),
            ],
            out_specs=moving(height),
            scratch_shapes=[VM((height, 2 * count), jnp.bfloat16)] * 2
            + [VM((2 * count, tile), jnp.bfloat16)] * 2,
        ),
        compiler_params=pltpu.CompilerParams(dimension_semantics=("arbitrary",), vmem_limit_bytes=LIMIT),
    )(offsets, left, projected, samples, values, diag, mask)


def solution(mesh):
    in_specs = (P(None, "col"), P("row", "col"), P("row"), P())
    out_specs = P("row", "col")
    return jax.shard_map(
        per_device, mesh=mesh, in_specs=in_specs, out_specs=out_specs, check_vma=False
    )
```

time: 372 us -> 212 us (0.57)
  Pallas kernels: 0 us -> 199 us
  waiting for transfers between devices: 179 us -> 0 us
  matrix products: 132 us -> 0 us
  local copies, waits for them, and re-layouts: 38.9 us -> 5.67 us
  between operations: 13.2 us -> 0.04 us
    pallas_call x0 -> x4, Pallas kernels: none -> 199 us  [the longest x1 105 us: per_device(): pl.pallas_call(functools.partial(reduce_kernel, lines, groups, per_group,...]
    psum x3 -> x0, waiting for transfers between devices: 179 us -> none  [the longest x1 170 us: per_device(): summed = lax.psum(partial_value, 'row')]
    dot_general x3 -> x0, matrix products: 132 us -> none  [the longest x1 61.8 us: per_device(): lax.dot_general(row_proj, samples, (((0,), (0,)), ((), ())), precision=la...]
    unnamed x5 -> x2, local copies, waits for them, and re-layouts: 34.1 us -> 0.82 us
    select_n x2 -> x0, other arithmetic: 4.66 us -> none  [the longest x1 2.35 us: per_device(): owned_proj = jnp.where(is_owner, local_proj, jnp.float32(0.0))]
  transfers between devices with their start and end apart: 3 -> 0, of which waited for: 3 -> 0; matrix products, arithmetic and copies ran while one was open for 19% -> 0% of each run, Pallas kernels for 0% -> 0%
where the time goes in v1:
time: 212 us; the launch traced here: 208 us
  Pallas kernels  199 us (94%)
  local copies, waits for them, and re-layouts  5.67 us (3%)
  other arithmetic  3.12 us (1%)
    pallas_call x1, Pallas kernels, per_device(): pl.pallas_call(functools.partial(reduce_kernel, lines, groups, per_group,...  105 us
    pallas_call x1, Pallas kernels, per_device(): pl.pallas_call(update_kernel, out_shape=jax.ShapeDtypeStruct((height, ord...  42 us
    pallas_call x1, Pallas kernels, per_device(): pl.pallas_call(project_kernel, out_shape=jax.ShapeDtypeStruct((count, ord...  27.4 us
    pallas_call x1, Pallas kernels, per_device(): pl.pallas_call(functools.partial(fetch_kernel, groups, per_group), out_sh...  24.3 us

profile of v1, /device:TPU:30, one launch (start us, length us, event | category | flops | bytes accessed | tf_op | source)
XLA Modules:
  0.0 207.6 jit_solution(9524393329838664502)
XLA Ops:
  0.0 0.6 pad_add_fusion.offset_ref
  0.6 0.8 dynamic-slice_convert_fusion
  1.4 0.1 broadcast_bitcast_fusion
  1.5 0.7 copy.11
  2.2 1.7 copy.7.diag_ref
  4.0 24.3 %shard_map.46.rows_ref = f32[256,1024]{1,0:T(8,128)} custom-call(f32[256,8192]{1,0:T(8,128)} %samples_ref.3), custom_call_target="tpu_custom_call" | custom-call | tf_op jit(solution)/shard_map/pallas_call | solution.py:417
  28.3 1.6 copy.8
  29.8 27.4 %shard_map.47.part_ref = f32[256,8192]{1,0:T(8,128)} custom-call(s32[2]{0:T(128)} %pad_add_fusion.offset_ref, f32[256,1024]{1,0:T(8,128)} %shard_map.46.rows_ref, f32[1024,8192]{1,0:T(8,128)} %values_ref.3, f32[1024,1]{1,0:T(8,128)} %copy.7.diag_ref, f32[4,8192]{1,0:T(4,128)} %bitcast.8), custom_call_target="tpu_custom_call" | custom-call | tf_op jit(solution)/shard_map/pallas_call | solution.py:435
  57.2 105.1 %shard_map.48 = (f32[256,8192]{1,0:T(8,128)}, f32[256,1024]{1,0:T(8,128)}) custom-call(f32[256,8192]{1,0:T(8,128)} %shard_map.47.part_ref), custom_call_target="tpu_custom_call" | custom-call | tf_op jit(solution)/shard_map/pallas_call | solution.py:452
  162.3 1.6 copy.9
  163.9 1.7 maximum_bitcast_fusion.left_ref
  165.6 42.0 %shard_map.49 = f32[1024,8192]{1,0:T(8,128)} custom-call(s32[2]{0:T(128)} %pad_add_fusion.offset_ref, f32[1024,512]{1,0:T(8,128)} %maximum_bitcast_fusion.left_ref, f32[256,8192]{1,0:T(8,128)} %get-tuple-element.8.proj_ref, f32[256,8192]{1,0:T(8,128)} %samples_ref.3, f32[1024,8192]{1,0:T(8,128)} %values_ref.3, f32[1024,1]{1,0:T(8,128)} %copy.7.diag_ref, ...), custom_call_target="tpu_custom_call" | custom-call | tf_op jit(solution)/shard_map/pallas_call | solution.py:468

commit v2 on v1

v2 whole, which is shorter than its diff:
```python
import functools

import jax
import jax.numpy as jnp
from jax import lax
from jax.experimental import pallas as pl
from jax.experimental.pallas import tpu as pltpu
from jax.sharding import PartitionSpec as P

step_size = 8.0
penalty = 0.05
MESH = pl.DeviceIdType.MESH
VM = pltpu.VMEM
LIMIT = 60 * 1024 * 1024


def split(x):
    high = x.astype(jnp.bfloat16)
    low = (x - high.astype(jnp.float32)).astype(jnp.bfloat16)
    return high, low


def dot(a, b):
    return jnp.dot(a, b, preferred_element_type=jnp.float32)


def on_diagonal(row_at, col_at, shape):
    rows = lax.broadcasted_iota(jnp.int32, shape, 0) + row_at
    cols = lax.broadcasted_iota(jnp.int32, shape, 1) + col_at
    return rows == cols


def crosses(row_at, col_at, shape):
    return jnp.logical_and(row_at < col_at + shape[1], col_at < row_at + shape[0])


def update_kernel(
    offset_ref, left_ref, proj_ref, samples_ref, values_ref, diag_ref, mask_ref, out_ref, lefts, rights
):
    step = pl.program_id(0)
    count = samples_ref.shape[0]
    parts = mask_ref.shape[0]
    height = values_ref.shape[0] // parts
    tile = values_ref.shape[1]
    both = 2 * count

    @pl.when(step == 0)
    def _():
        high, low = split(left_ref[...].T * (0.5 * step_size / count))
        lefts[:, :both] = high
        lefts[:, both : 2 * both] = high
        lefts[:, 2 * both :] = low

    for at, ref in ((0, proj_ref), (count, samples_ref)):
        high, low = split(ref[...])
        rights[at : at + count, :] = high
        rights[both + at : both + at + count, :] = low
        rights[2 * both + at : 2 * both + at + count, :] = high
    limit = step_size * penalty
    for part in range(parts):
        rows = pl.ds(part * height, height)
        row_at, col_at = offset_ref[0] + part * height, offset_ref[1] + step * tile
        hit = crosses(row_at, col_at, (height, tile))
        cross = dot(lefts[rows, :], rights[...])
        stepped = values_ref[rows, :] * mask_ref[part : part + 1, :] - cross
        out_ref[rows, :] = stepped - jnp.clip(stepped, -limit, limit)

        @pl.when(hit)
        def _(rows=rows, row_at=row_at, col_at=col_at):
            diag = diag_ref[rows, :]
            product = dot(lefts[rows, :], rights[...])
            diagonal = on_diagonal(row_at, col_at, product.shape)
            out_ref[rows, :] = jnp.where(diagonal, diag - product + step_size / diag, out_ref[rows, :])


def reduce_kernel(
    lines, groups, per_group, spans, deeps, samples_ref, values_ref, diag_ref, mask_ref, out_ref, left_ref, *scratch
):
    chunks = spans * deeps
    (core_in, y_in, a_right, a_left, b_right, b_left, y_right, y_left) = scratch[:8]
    send, recv = scratch[8], scratch[9]
    part_ref, held, lefts, rights, held_sem, fetch_send, fetch_sem = scratch[10:]
    row, col = lax.axis_index("row"), lax.axis_index("col")
    core, side, line = row % 2, row // 2 % 2, row // 4
    last = lines - 1
    core_mate = row + 1 - 2 * core
    y_mate = row + 2 - 4 * side
    up, down = row + 4, row - 4
    samples, columns = part_ref.shape
    order = columns // spans
    deep = samples // deeps
    half, quarter, eighth, sixteenth = order // 2, order // 4, order // 8, order // 16
    has_up, has_down = line < last, line > 0
    owner = row // per_group
    width = left_ref.shape[1]
    rows_ref, proj_ref = left_ref.at[:samples, :], left_ref.at[samples:, :]
    slice_at = pl.multiple_of(row % per_group * width, width)

    barrier = pltpu.get_barrier_semaphore()

    def greet(target):
        pl.semaphore_signal(barrier, inc=1, device_id=target, device_id_type=MESH)

    greet((core_mate, col))
    greet((y_mate, col))
    pl.when(has_up)(lambda: greet((up, col)))
    pl.when(has_down)(lambda: greet((down, col)))
    for shift in range(1, groups):
        greet((row, lax.rem(col + shift, groups)))
    ends = jnp.where(has_up, 1, 0) + jnp.where(has_down, 1, 0)
    pl.semaphore_wait(barrier, 2 + groups - 1 + ends)

    def span(at, size):
        return pl.ds(pl.multiple_of(at, sixteenth), size)

    def rows_of(q):
        return pl.ds(pl.multiple_of(q % deeps * deep, deep), deep)

    def base(q):
        return q // deeps * order

    def a_at(q, k, v):
        return base(q) + k * half + v * eighth

    def b_at(q, k):
        return base(q) + k * half + quarter

    def copy(kind, q, source, target, device, landing=None):
        return pltpu.make_async_remote_copy(
            src_ref=source,
            dst_ref=target,
            send_sem=send.at[kind, q],
            recv_sem=recv.at[kind if landing is None else landing, q],
            device_id=device,
            device_id_type=MESH,
        )

    def whole(ref, q):
        return ref.at[q]

    def out_at(q, at, size):
        return out_ref.at[rows_of(q), span(at, size)]

    def c_core(q):
        return copy(0, q, part_ref.at[rows_of(q), span(base(q) + (1 - core) * half, half)], whole(core_in, q), (core_mate, col))

    def c_y(q):
        return copy(1, q, core_in.at[q, :, span((1 - side) * eighth, eighth)], whole(y_in, q), (y_mate, col))

    def c_b_right(q, first):
        source = core_in.at[q, :, span(quarter, eighth)] if first else whole(b_right, q)
        return copy(2, q, source, whole(b_right, q), (up, col))

    def c_b_left(q, first):
        source = core_in.at[q, :, span(quarter + eighth, eighth)] if first else whole(b_left, q)
        return copy(3, q, source, whole(b_left, q), (down, col))

    def c_a_right(q, first):
        source = y_in.at[q, :, span(0, sixteenth)] if first else whole(a_right, q)
        return copy(4, q, source, whole(a_right, q), (up, col))

    def c_a_left(q, first):
        source = y_in.at[q, :, span(sixteenth, sixteenth)] if first else whole(a_left, q)
        return copy(5, q, source, whole(a_left, q), (down, col))

    def c_y_right(q):
        return copy(6, q, whole(b_right, q), whole(y_right, q), (y_mate, col))

    def c_y_left(q):
        return copy(7, q, whole(b_left, q), whole(y_left, q), (y_mate, col))

    def spread(kind, q, at, size, target):
        return copy(kind, q, out_at(q, at, size), out_at(q, at, size), (target, col))

    def b_piece(q, flow):
        return b_at(q, core) + flow * eighth, eighth

    def a_piece(q, flow, v):
        return a_at(q, core, v) + flow * sixteenth, sixteenth

    def c_b_back(q, flow):
        return spread(8 + flow, q, *b_piece(q, flow), (down, up)[flow])

    def c_a_back(q, flow):
        return spread(10 + flow, q, *a_piece(q, flow, side), (down, up)[flow])

    def c_y_back(q, flow):
        return spread(12 + flow, q, *a_piece(q, flow, side), y_mate)

    def y_back_arrival(q, flow):
        return spread(12 + flow, q, *a_piece(q, flow, 1 - side), y_mate)

    def c_core_back(q, index, at, size):
        return copy(14 + index, q, out_at(q, at, size), out_at(q, at, size), (core_mate, col), 14 + index)

    def core_arrival(q, index, at, size):
        other = at - core * half + (1 - core) * half
        return c_core_back(q, index, other, size)

    def pieces(q):
        for flow in range(2):
            yield flow, *b_piece(q, flow)
            yield 2 + flow, *a_piece(q, flow, side)
            yield 4 + flow, *a_piece(q, flow, 1 - side)

    def core_pieces_in(q):
        for index, at, size in pieces(q):
            core_arrival(q, index, at, size).wait_recv()

    def c_proj(q, shift):
        d = q % deeps
        return copy(
            20 + shift,
            d,
            out_ref.at[rows_of(q), pl.ds(slice_at, width)],
            proj_ref.at[rows_of(q), :],
            (row, lax.rem(col + shift, groups)),
            21,
        )

    def at_stage(t, offset, condition, action):
        q = t - offset
        live = jnp.logical_and(q >= 0, q < chunks)
        if condition is not None:
            live = jnp.logical_and(live, condition)
        pl.when(live)(lambda: action(jnp.clip(q, 0, chunks - 1)))

    def begin(q):
        c_core(q).wait_recv()
        rows = rows_of(q)
        core_in[q] = core_in[q] + part_ref[rows, span(base(q) + core * half, half)]
        c_y(q).start()
        pl.when(line == 0)(lambda: c_b_right(q, True).start())
        pl.when(line == last)(lambda: c_b_left(q, True).start())

    def after_y(q):
        c_y(q).wait_recv()
        y_in[q] = y_in[q] + core_in[q, :, span(side * eighth, eighth)]
        pl.when(line == 0)(lambda: c_a_right(q, True).start())
        pl.when(line == last)(lambda: c_a_left(q, True).start())

    def b_hop(q, flow):
        ref, make = (b_right, c_b_right) if flow == 0 else (b_left, c_b_left)
        make(q, False).wait_recv()
        ref[q] = ref[q] + core_in[q, :, span(quarter + flow * eighth, eighth)]
        going = has_up if flow == 0 else has_down
        pl.when(going)(lambda: make(q, False).start())
        pl.when(jnp.logical_not(going))(lambda: (c_y_right if flow == 0 else c_y_left)(q).start())

    def done_a(q, flow, forward):
        pl.when(forward)(lambda: c_a_back(q, flow).start())
        c_y_back(q, flow).start()
        c_core_back(q, 2 + flow, *a_piece(q, flow, side)).start()

    def done_b(q, flow, forward):
        pl.when(forward)(lambda: c_b_back(q, flow).start())
        c_core_back(q, flow, *b_piece(q, flow)).start()

    def a_hop(q, flow):
        ref, make = (a_right, c_a_right) if flow == 0 else (a_left, c_a_left)
        make(q, False).wait_recv()
        rows = rows_of(q)
        value = ref[q] + y_in[q, :, span(flow * sixteenth, sixteenth)]
        going = has_up if flow == 0 else has_down

        @pl.when(going)
        def _():
            ref[q] = value
            make(q, False).start()

        @pl.when(jnp.logical_not(going))
        def _():
            out_ref[rows, span(*a_piece(q, flow, side))] = value
            done_a(q, flow, True)

    def b_end(q, flow):
        ref, other, make = (b_right, y_right, c_y_right) if flow == 0 else (b_left, y_left, c_y_left)
        make(q).wait_recv()
        rows = rows_of(q)
        out_ref[rows, span(*b_piece(q, flow))] = ref[q] + other[q]
        done_b(q, flow, True)

    def back(q, flow):
        forward = has_down if flow == 0 else has_up
        c_a_back(q, flow).wait_recv()
        done_a(q, flow, forward)
        c_b_back(q, flow).wait_recv()
        done_b(q, flow, forward)

    def y_gather(q, flow):
        y_back_arrival(q, flow).wait_recv()
        c_core_back(q, 4 + flow, *a_piece(q, flow, 1 - side)).start()

    def finish(q):
        core_pieces_in(q)
        rows = rows_of(q)

        @pl.when(jnp.logical_and(col == owner, q // deeps == slice_at // order))
        def _():
            for shift in range(1, groups):
                c_proj(q, shift).start()
            proj_ref[rows, :] = out_ref[rows, pl.ds(slice_at, width)]

    height = values_ref.shape[0]
    parts = mask_ref.shape[0]
    block = height // parts
    tile = order // deeps

    def load(i):
        slot = i % 2
        at = pl.multiple_of(i * tile, tile)
        return pltpu.make_async_copy(values_ref.at[:, pl.ds(at, tile)], held.at[slot], held_sem.at[slot])

    load(0).start()
    load(1).start()
    mine = samples_ref.at[:, pl.ds(slice_at, width)]

    def fetch(shift):
        return pltpu.make_async_remote_copy(
            src_ref=mine,
            dst_ref=rows_ref,
            send_sem=fetch_send.at[shift],
            recv_sem=fetch_sem.at[0],
            device_id=(row, lax.rem(col + shift, groups)),
            device_id_type=MESH,
        )

    @pl.when(col == owner)
    def _():
        for shift in range(1, groups):
            fetch(shift).start()
        own = pltpu.make_async_copy(mine, rows_ref, fetch_sem.at[1])
        own.start()
        own.wait()

    @pl.when(col != owner)
    def _():
        fetch(1).wait_recv()

    high, low = split(rows_ref[...])
    lefts[:, :height] = high
    lefts[:, height : 2 * height] = high
    lefts[:, 2 * height :] = low

    def project(i):
        load(i).wait()
        slot = i % 2
        cols = pl.ds(pl.multiple_of(i * tile, tile), tile)
        for index in range(parts):
            begin_at = index * block
            rows = pl.ds(begin_at, block)
            row_at, col_at = row * height + begin_at, col * columns + i * tile
            hit = crosses(row_at, col_at, (block, tile))

            def put(omega, begin_at=begin_at):
                high, low = split(omega)
                rights[begin_at : begin_at + block, :] = high
                rights[height + begin_at : height + begin_at + block, :] = low
                rights[2 * height + begin_at : 2 * height + begin_at + block, :] = high

            masked = held[slot, rows, :] * mask_ref[index : index + 1, cols]
            put(masked)

            @pl.when(hit)
            def _(rows=rows, row_at=row_at, col_at=col_at, put=put, index=index):
                again = held[slot, rows, :] * mask_ref[index : index + 1, cols]
                put(jnp.where(on_diagonal(row_at, col_at, again.shape), diag_ref[rows, :], again))

        part_ref[:, cols] = dot(lefts[...], rights[...])
        pl.when(i + 2 < chunks)(lambda: load(i + 2).start())

        @pl.when(i % deeps == deeps - 1)
        def _():
            for index in range(deeps):
                c_core(i - (deeps - 1) + index).start()

    total = 2 * lines + 2 + deeps

    @pl.loop(0, chunks + total)
    def _(t):
        at_stage(t, 0, None, project)
        at_stage(t - deeps, 0, None, begin)
        at_stage(t - deeps, 1, None, after_y)
        at_stage(t - deeps, line, has_down, lambda q: b_hop(q, 0))
        at_stage(t - deeps, last - line, has_up, lambda q: b_hop(q, 1))
        at_stage(t - deeps, 1 + line, has_down, lambda q: a_hop(q, 0))
        at_stage(t - deeps, lines - line, has_up, lambda q: a_hop(q, 1))
        at_stage(t - deeps, lines, line == last, lambda q: b_end(q, 0))
        at_stage(t - deeps, lines, line == 0, lambda q: b_end(q, 1))
        at_stage(t - deeps, lines + last - line, has_up, lambda q: back(q, 0))
        at_stage(t - deeps, lines + line, has_down, lambda q: back(q, 1))
        at_stage(t - deeps, lines + last - line + 1, None, lambda q: y_gather(q, 0))
        at_stage(t - deeps, lines + line + 1, None, lambda q: y_gather(q, 1))
        at_stage(t - deeps, 2 * lines + 1, None, finish)

    @pl.loop(0, chunks)
    def _(q):
        c_core(q).wait_send()
        c_y(q).wait_send()
        pl.when(has_up)(lambda: c_b_right(q, False).wait_send())
        pl.when(has_down)(lambda: c_b_left(q, False).wait_send())
        pl.when(has_up)(lambda: c_a_right(q, False).wait_send())
        pl.when(has_down)(lambda: c_a_left(q, False).wait_send())
        pl.when(line == last)(lambda: c_y_right(q).wait_send())
        pl.when(line == 0)(lambda: c_y_left(q).wait_send())
        for flow, forward in ((0, has_down), (1, has_up)):
            pl.when(forward)(lambda flow=flow: c_b_back(q, flow).wait_send())
            pl.when(forward)(lambda flow=flow: c_a_back(q, flow).wait_send())
            c_y_back(q, flow).wait_send()
        for index, at, size in pieces(q):
            c_core_back(q, index, at, size).wait_send()

    @pl.when(col == owner)
    def _():
        for shift in range(1, groups):
            fetch(shift).wait_send()

    @pl.loop(0, deeps)
    def _(q):
        @pl.when(col == owner)
        def _():
            for shift in range(1, groups):
                c_proj(q, shift).wait_send()

        @pl.when(col != owner)
        def _():
            c_proj(q, 1).wait_recv()


def per_device(samples, values, diag_entries, block_mask):
    height, order = values.shape
    count = samples.shape[0]
    groups = lax.axis_size("col")
    lines = lax.axis_size("row") // 4
    per_group = order // height
    row_at = lax.axis_index("row") * height
    col_at = lax.axis_index("col") * order
    block = groups * order // block_mask.shape[0]
    tile_mask = lax.dynamic_slice(
        block_mask, (row_at // block, col_at // block), (height // block, order // block)
    )
    mask = jnp.repeat(tile_mask.astype(jnp.float32), block, axis=1)
    diag = diag_entries[:, None]
    offsets = jnp.stack([row_at, col_at]).astype(jnp.int32)
    anywhere = pl.BlockSpec(memory_space=pl.ANY)
    in_vmem = pl.BlockSpec(memory_space=VM)
    parts = mask.shape[0]
    tile = 2 * block
    spans = max(1, order // (16 * 128))
    deeps = order // spans // tile
    chunks = spans * deeps
    deep = count // deeps
    wide = order // spans
    eighth, sixteenth = wide // 8, wide // 16
    widths = [wide // 2, eighth, sixteenth, sixteenth, eighth, eighth, eighth, eighth]
    kinds = 21 + groups
    projected, left = pl.pallas_call(
        functools.partial(reduce_kernel, lines, groups, per_group, spans, deeps),
        out_shape=(
            jax.ShapeDtypeStruct((count, order), jnp.float32),
            jax.ShapeDtypeStruct((2 * count, height), jnp.float32),
        ),
        in_specs=[anywhere, anywhere, in_vmem, in_vmem],
        out_specs=(in_vmem, in_vmem),
        scratch_shapes=[VM((chunks, deep, w), jnp.float32) for w in widths]
        + [pltpu.SemaphoreType.DMA((kinds, chunks)), pltpu.SemaphoreType.DMA((kinds, chunks))]
        + [
            VM((count, order), jnp.float32),
            VM((2, height, tile), jnp.float32),
            VM((count, 3 * height), jnp.bfloat16),
            VM((3 * height, tile), jnp.bfloat16),
            pltpu.SemaphoreType.DMA((2,)),
            pltpu.SemaphoreType.DMA((groups,)),
            pltpu.SemaphoreType.DMA((2,)),
        ],
        compiler_params=pltpu.CompilerParams(
            collective_id=1, has_side_effects=True, vmem_limit_bytes=LIMIT
        ),
    )(samples, values, diag, mask)

    grid = order // tile
    fixed = lambda shape: pl.BlockSpec(shape, lambda i, s: (0, 0))
    moving = lambda rows: pl.BlockSpec((rows, tile), lambda i, s: (0, i))
    return pl.pallas_call(
        update_kernel,
        out_shape=jax.ShapeDtypeStruct((height, order), jnp.float32),
        grid_spec=pltpu.PrefetchScalarGridSpec(
            num_scalar_prefetch=1,
            grid=(grid,),
            in_specs=[
                fixed((2 * count, height)),
                moving(count),
                moving(count),
                moving(height),
                fixed((height, 1)),
                moving(parts),
            ],
            out_specs=moving(height),
            scratch_shapes=[
                VM((height, 6 * count), jnp.bfloat16),
                VM((6 * count, tile), jnp.bfloat16),
            ],
        ),
        compiler_params=pltpu.CompilerParams(dimension_semantics=("arbitrary",), vmem_limit_bytes=LIMIT),
    )(offsets, left, projected, samples, values, diag, mask)


def solution(mesh):
    in_specs = (P(None, "col"), P("row", "col"), P("row"), P())
    out_specs = P("row", "col")
    return jax.shard_map(
        per_device, mesh=mesh, in_specs=in_specs, out_specs=out_specs, check_vma=False
    )
```

time: 212 us -> 200 us (0.943); the launches traced: 208 us -> 199 us
  Pallas kernels: 199 us -> 195 us
  local copies, waits for them, and re-layouts: 5.67 us -> 2.56 us
    pallas_call x2 -> x0, Pallas kernels: 51.7 us -> none  [the longest x1 27.4 us: per_device(): pl.pallas_call(project_kernel, out_shape=jax.ShapeDtypeStruct((count, ord...]
    pallas_call x1, Pallas kernels: 105 us -> 148 us  [per_device(): pl.pallas_call(functools.partial(reduce_kernel, lines, groups, per_group,...]
    pallas_call x1, Pallas kernels: 42 us -> 47.9 us  [per_device(): pl.pallas_call(update_kernel, out_shape=jax.ShapeDtypeStruct((height, ord...]
    pallas_call x2 -> x0, local copies, waits for them, and re-layouts: 3.11 us -> none  [the longest x1 1.56 us: per_device(): pl.pallas_call(functools.partial(fetch_kernel, groups, per_group), out_sh...]
where the time goes in v2:
time: 200 us; the launch traced here: 199 us
  Pallas kernels  195 us (98%)
  local copies, waits for them, and re-layouts  2.56 us (1%)
    pallas_call x1, Pallas kernels, per_device(): pl.pallas_call(functools.partial(reduce_kernel, lines, groups, per_group,...  148 us
    pallas_call x1, Pallas kernels, per_device(): pl.pallas_call(update_kernel, out_shape=jax.ShapeDtypeStruct((height, ord...  47.9 us

profile of v2, /device:TPU:30, one launch (start us, length us, event | category | flops | bytes accessed | tf_op | source)
XLA Modules:
  0.0 199.5 jit_solution(14913321495706729164)
XLA Ops:
  0.0 0.6 pad_add_fusion.offset_ref
  0.6 0.8 dynamic-slice_convert_fusion
  1.4 0.1 broadcast_bitcast_fusion
  1.5 0.7 copy.7
  2.2 1.7 copy.5.diag_ref
  4.0 147.6 %shard_map.46 = (f32[256,8192]{1,0:T(8,128)}, f32[512,1024]{1,0:T(8,128)}) custom-call(f32[256,8192]{1,0:T(8,128)} %samples_ref.3, f32[1024,8192]{1,0:T(8,128)} %values_ref.3, f32[1024,1]{1,0:T(8,128)} %copy.5.diag_ref, f32[4,8192]{1,0:T(4,128)} %bitcast.6), custom_call_target="tpu_custom_call" | custom-call | tf_op jit(solution)/shard_map/pallas_call | solution.py:457
  151.6 47.9 %shard_map.47 = f32[1024,8192]{1,0:T(8,128)} custom-call(s32[2]{0:T(128)} %pad_add_fusion.offset_ref, f32[512,1024]{1,0:T(8,128)} %get-tuple-element.7.left_ref, f32[256,8192]{1,0:T(8,128)} %get-tuple-element.8.proj_ref, f32[256,8192]{1,0:T(8,128)} %samples_ref.3, f32[1024,8192]{1,0:T(8,128)} %values_ref.3, f32[1024,1]{1,0:T(8,128)} %copy.5.diag_ref, ...), custom_call_target="tpu_custom_call" | custom-call | tf_op jit(solution)/shard_map/pallas_call | solution.py:484

commit v3 on v2

--- a/solution.py
+++ b/solution.py
@@ -30,47 +30,57 @@
     return rows == cols
 
 
+def masked(mask_ref, values, row_at, col_at, block):
+    pieces = [
+        values[:, at : at + block] * mask_ref[row_at // block, (col_at + at) // block].astype(jnp.float32)
+        for at in range(0, values.shape[1], block)
+    ]
+    return jnp.concatenate(pieces, axis=1)
+
+
 def crosses(row_at, col_at, shape):
     return jnp.logical_and(row_at < col_at + shape[1], col_at < row_at + shape[0])
 
 
-def update_kernel(
-    offset_ref, left_ref, proj_ref, samples_ref, values_ref, diag_ref, mask_ref, out_ref, lefts, rights
-):
+def update_kernel(left_ref, proj_ref, samples_ref, values_ref, diag_ref, mask_ref, out_ref, lefts, rights):
     step = pl.program_id(0)
     count = samples_ref.shape[0]
-    parts = mask_ref.shape[0]
-    height = values_ref.shape[0] // parts
-    tile = values_ref.shape[1]
+    height, tile = values_ref.shape
     both = 2 * count
+    block = lax.axis_size("col") * pl.num_programs(0) * tile // mask_ref.shape[0]
+    row_at = lax.axis_index("row") * height
+    col_at = (lax.axis_index("col") * pl.num_programs(0) + step) * tile
 
     @pl.when(step == 0)
     def _():
         high, low = split(left_ref[...].T * (0.5 * step_size / count))
         lefts[:, :both] = high
-        lefts[:, both : 2 * both] = high
-        lefts[:, 2 * both :] = low
+        lefts[:, both:] = low
 
     for at, ref in ((0, proj_ref), (count, samples_ref)):
         high, low = split(ref[...])
         rights[at : at + count, :] = high
         rights[both + at : both + at + count, :] = low
-        rights[2 * both + at : 2 * both + at + count, :] = high
     limit = step_size * penalty
-    for part in range(parts):
-        rows = pl.ds(part * height, height)
-        row_at, col_at = offset_ref[0] + part * height, offset_ref[1] + step * tile
-        hit = crosses(row_at, col_at, (height, tile))
-        cross = dot(lefts[rows, :], rights[...])
-        stepped = values_ref[rows, :] * mask_ref[part : part + 1, :] - cross
-        out_ref[rows, :] = stepped - jnp.clip(stepped, -limit, limit)
-
-        @pl.when(hit)
-        def _(rows=rows, row_at=row_at, col_at=col_at):
-            diag = diag_ref[rows, :]
-            product = dot(lefts[rows, :], rights[...])
-            diagonal = on_diagonal(row_at, col_at, product.shape)
-            out_ref[rows, :] = jnp.where(diagonal, diag - product + step_size / diag, out_ref[rows, :])
+
+    def update(hit):
+        for begin in range(0, height, block):
+            rows = pl.ds(begin, block)
+            left_high, left_low = lefts[rows, :both], lefts[rows, both:]
+            cross = dot(left_high, rights[:both, :]) + dot(left_low, rights[:both, :]) + dot(left_high, rights[both:, :])
+            omega = masked(mask_ref, values_ref[rows, :], row_at + begin, col_at, block)
+            stepped = omega - cross
+            new = stepped - jnp.clip(stepped, -limit, limit)
+            if hit:
+                diag = diag_ref[:, pl.ds(pl.multiple_of(col_at - row_at, tile), tile)]
+                new = jnp.where(
+                    on_diagonal(row_at + begin, col_at, new.shape), diag - cross + step_size / diag, new
+                )
+            out_ref[rows, :] = new
+
+    hit = crosses(row_at, col_at, (height, tile))
+    pl.when(hit)(lambda: update(True))
+    pl.when(jnp.logical_not(hit))(lambda: update(False))
 
 
 def reduce_kernel(
@@ -302,8 +312,7 @@
             proj_ref[rows, :] = out_ref[rows, pl.ds(slice_at, width)]
 
     height = values_ref.shape[0]
-    parts = mask_ref.shape[0]
-    block = height // parts
+    block = groups * columns // mask_ref.shape[0]
     tile = order // deeps
 
     def load(i):
@@ -346,27 +355,22 @@
         load(i).wait()
         slot = i % 2
         cols = pl.ds(pl.multiple_of(i * tile, tile), tile)
-        for index in range(parts):
-            begin_at = index * block
-            rows = pl.ds(begin_at, block)
-            row_at, col_at = row * height + begin_at, col * columns + i * tile
-            hit = crosses(row_at, col_at, (block, tile))
-
-            def put(omega, begin_at=begin_at):
+        row_at, col_at = row * height, col * columns + i * tile
+        hit = crosses(row_at, col_at, (height, tile))
+
+        def put(hit):
+            for begin_at in range(0, height, block):
+                omega = masked(mask_ref, held[slot, pl.ds(begin_at, block), :], row_at + begin_at, col_at, block)
+                if hit:
+                    diag = diag_ref[:, pl.ds(pl.multiple_of(col_at - row_at, tile), tile)]
+                    omega = jnp.where(on_diagonal(row_at + begin_at, col_at, omega.shape), diag, omega)
                 high, low = split(omega)
                 rights[begin_at : begin_at + block, :] = high
                 rights[height + begin_at : height + begin_at + block, :] = low
-                rights[2 * height + begin_at : 2 * height + begin_at + block, :] = high
-
-            masked = held[slot, rows, :] * mask_ref[index : index + 1, cols]
-            put(masked)
-
-            @pl.when(hit)
-            def _(rows=rows, row_at=row_at, col_at=col_at, put=put, index=index):
-                again = held[slot, rows, :] * mask_ref[index : index + 1, cols]
-                put(jnp.where(on_diagonal(row_at, col_at, again.shape), diag_ref[rows, :], again))
-
-        part_ref[:, cols] = dot(lefts[...], rights[...])
+
+        pl.when(hit)(lambda: put(True))
+        pl.when(jnp.logical_not(hit))(lambda: put(False))
+        part_ref[:, cols] = dot(lefts[:, : 2 * height], rights[...]) + dot(lefts[:, 2 * height :], rights[:height, :])
         pl.when(i + 2 < chunks)(lambda: load(i + 2).start())
 
         @pl.when(i % deeps == deeps - 1)
@@ -433,18 +437,11 @@
     groups = lax.axis_size("col")
     lines = lax.axis_size("row") // 4
     per_group = order // height
-    row_at = lax.axis_index("row") * height
-    col_at = lax.axis_index("col") * order
     block = groups * order // block_mask.shape[0]
-    tile_mask = lax.dynamic_slice(
-        block_mask, (row_at // block, col_at // block), (height // block, order // block)
-    )
-    mask = jnp.repeat(tile_mask.astype(jnp.float32), block, axis=1)
-    diag = diag_entries[:, None]
-    offsets = jnp.stack([row_at, col_at]).astype(jnp.int32)
+    diag = diag_entries[None, :]
     anywhere = pl.BlockSpec(memory_space=pl.ANY)
+    in_smem = pl.BlockSpec(memory_space=pltpu.SMEM)
     in_vmem = pl.BlockSpec(memory_space=VM)
-    parts = mask.shape[0]
     tile = 2 * block
     spans = max(1, order // (16 * 128))
     deeps = order // spans // tile
@@ -460,7 +457,7 @@
             jax.ShapeDtypeStruct((count, order), jnp.float32),
             jax.ShapeDtypeStruct((2 * count, height), jnp.float32),
         ),
-        in_specs=[anywhere, anywhere, in_vmem, in_vmem],
+        in_specs=[anywhere, anywhere, in_vmem, in_smem],
         out_specs=(in_vmem, in_vmem),
         scratch_shapes=[VM((chunks, deep, w), jnp.float32) for w in widths]
         + [pltpu.SemaphoreType.DMA((kinds, chunks)), pltpu.SemaphoreType.DMA((kinds, chunks))]
@@ -468,7 +465,7 @@
             VM((count, order), jnp.float32),
             VM((2, height, tile), jnp.float32),
             VM((count, 3 * height), jnp.bfloat16),
-            VM((3 * height, tile), jnp.bfloat16),
+            VM((2 * height, tile), jnp.bfloat16),
             pltpu.SemaphoreType.DMA((2,)),
             pltpu.SemaphoreType.DMA((groups,)),
             pltpu.SemaphoreType.DMA((2,)),
@@ -476,33 +473,31 @@
         compiler_params=pltpu.CompilerParams(
             collective_id=1, has_side_effects=True, vmem_limit_bytes=LIMIT
         ),
-    )(samples, values, diag, mask)
-
+    )(samples, values, diag, block_mask)
+
+    tile = min(4 * block, height)
     grid = order // tile
-    fixed = lambda shape: pl.BlockSpec(shape, lambda i, s: (0, 0))
-    moving = lambda rows: pl.BlockSpec((rows, tile), lambda i, s: (0, i))
+    fixed = lambda shape: pl.BlockSpec(shape, lambda i: (0, 0))
+    moving = lambda rows: pl.BlockSpec((rows, tile), lambda i: (0, i))
     return pl.pallas_call(
         update_kernel,
         out_shape=jax.ShapeDtypeStruct((height, order), jnp.float32),
-        grid_spec=pltpu.PrefetchScalarGridSpec(
-            num_scalar_prefetch=1,
-            grid=(grid,),
-            in_specs=[
-                fixed((2 * count, height)),
-                moving(count),
-                moving(count),
-                moving(height),
-                fixed((height, 1)),
-                moving(parts),
-            ],
-            out_specs=moving(height),
-            scratch_shapes=[
-                VM((height, 6 * count), jnp.bfloat16),
-                VM((6 * count, tile), jnp.bfloat16),
-            ],
-        ),
+        grid=(grid,),
+        in_specs=[
+            fixed((2 * count, height)),
+            moving(count),
+            moving(count),
+            moving(height),
+            fixed((1, height)),
+            in_smem,
+        ],
+        out_specs=moving(height),
+        scratch_shapes=[
+            VM((height, 4 * count), jnp.bfloat16),
+            VM((4 * count, tile), jnp.bfloat16),
+        ],
         compiler_params=pltpu.CompilerParams(dimension_semantics=("arbitrary",), vmem_limit_bytes=LIMIT),
-    )(offsets, left, projected, samples, values, diag, mask)
+    )(left, projected, samples, values, diag, block_mask)
 
 
 def solution(mesh):

time: 200 us -> 188 us (0.940)
  Pallas kernels: 195 us -> 186 us
  local copies, waits for them, and re-layouts: 2.56 us -> 0 us
    pallas_call x1, Pallas kernels: 47.9 us -> 39.1 us  [per_device(): pl.pallas_call(update_kernel, out_shape=jax.ShapeDtypeStruct((height, ord...]
where the time goes in v3:
time: 188 us; the launch traced here: 186 us
  Pallas kernels  186 us (99%)
    pallas_call x1, Pallas kernels, per_device(): pl.pallas_call(functools.partial(reduce_kernel, lines, groups, per_group,...  147 us
    pallas_call x1, Pallas kernels, per_device(): pl.pallas_call(update_kernel, out_shape=jax.ShapeDtypeStruct((height, ord...  39.1 us

profile of v3, /device:TPU:30, one launch (start us, length us, event | category | flops | bytes accessed | tf_op | source)
XLA Modules:
  0.0 186.1 jit_solution(15008198109340302755)
XLA Ops:
  0.0 147.0 %shard_map.46 = (f32[256,8192]{1,0:T(8,128)}, f32[512,1024]{1,0:T(8,128)}) custom-call(f32[256,8192]{1,0:T(8,128)} %samples_ref.3, f32[1024,8192]{1,0:T(8,128)} %values_ref.3, f32[1,1024]{1,0:T(1,128)} %bitcast.1, s32[64,64]{1,0:T(8,128)} %mask_ref.3), custom_call_target="tpu_custom_call" | custom-call | tf_op jit(solution)/shard_map/pallas_call | solution.py:454
  147.0 39.1 %shard_map.47 = f32[1024,8192]{1,0:T(8,128)} custom-call(f32[512,1024]{1,0:T(8,128)} %get-tuple-element.7.left_ref, f32[256,8192]{1,0:T(8,128)} %get-tuple-element.8.proj_ref, f32[256,8192]{1,0:T(8,128)} %samples_ref.3, f32[1024,8192]{1,0:T(8,128)} %values_ref.3, f32[1,1024]{1,0:T(1,128)} %bitcast.2, s32[64,64]{1,0:T(8,128)} %mask_ref.3), custom_call_target="tpu_custom_call" | custom-call | tf_op jit(solution)/shard_map/pallas_call | solution.py:482
